TPU v7x, 32 devices: a whole 2x2x4 slice. The times are simulated.
32 devices in a mesh: seq: 8 (over z, x), head: 4 (over y, core).
Axes of the slice: x: 2, y: 2, z: 4, core: 2. Of those that a mesh axis runs over, the one named last changes fastest.
Arguments:
- inputs: bfloat16 [3, 4096, 4096], P(None, 'seq', 'head'), may hold values from -11 to 11
- conv_weight: float32 [3, 3, 4096], P(None, None, 'head'), may hold values from -9 to 9
- gain: float32 [4096], P('head'), may hold values from 0.5 to 1.5
- cotangent: bfloat16 [4096, 4096], P('seq', 'head'), may hold values from -11 to 11
Outputs:
- output: bfloat16 [4096, 4096], P('seq', 'head')
- grad_inputs: bfloat16 [3, 4096, 4096], P(None, 'seq', 'head')
All inputs are finite; a program needn't handle non-finite values.
Results may differ from a plain program's by a relative error of at most 0.0078.
Values may be sent and summed in bfloat16 or wider, within the bound.
A program may use at most 128 MiB of HBM per device.

v0:
```python
import jax
import jax.numpy as jnp
from jax import lax
from jax.sharding import PartitionSpec as P

WIDTH = 4096
HEAD_DIM = 128
BLOCK = 512


def from_behind(x, axis, by):
    devices = lax.axis_size(axis)
    pairs = [(i, i + by) for i in range(devices) if 0 <= i + by < devices]
    return lax.ppermute(x, axis, pairs)


def entering(part, axis, combine, identity, reverse):
    count = lax.axis_size(axis)
    place = lax.axis_index(axis)
    ahead = count - 1 - place if reverse else place
    gathered = lax.all_gather(part, axis)
    state = jnp.zeros_like(part) + jnp.asarray(identity, part.dtype)

    def one(step, state):
        source = count - 1 - step if reverse else step
        return combine(state, lax.dynamic_index_in_dim(gathered, source, 0, False))

    return lax.fori_loop(0, ahead, one, state)


def add_states(earlier, later):
    return earlier + later


def body(inputs, conv_weight, gain, cotangent):
    row_count = inputs.shape[1]
    col_count = inputs.shape[2]
    tap_count = conv_weight.shape[1]
    local_heads = col_count // HEAD_DIM
    block_count = row_count // BLOCK
    left_rim = from_behind(inputs[:, row_count - (tap_count - 1) :, :], "seq", 1)
    extended = jnp.concatenate([left_rim, inputs], axis=1).astype(jnp.float32)
    conv_total = jnp.zeros((3, row_count, col_count), jnp.float32)
    for offset in range(tap_count):
        start_row = tap_count - 1 - offset
        conv_total = (
            conv_total
            + conv_weight[:, offset, None, :] * extended[:, start_row : start_row + row_count, :]
        )
    convolved = conv_total.astype(jnp.bfloat16)

    def by_blocks(array):
        return array.reshape(block_count, BLOCK, local_heads, HEAD_DIM)

    queries = by_blocks(convolved[0])
    key_rows = by_blocks(convolved[1])
    values = by_blocks(convolved[2])
    causal = lax.broadcasted_iota(jnp.int32, (BLOCK, BLOCK), 0) >= lax.broadcasted_iota(
        jnp.int32, (BLOCK, BLOCK), 1
    )
    block_states = jnp.einsum(
        "nshd,nshe->nhde", key_rows, values, preferred_element_type=jnp.float32
    )
    device_state = jnp.sum(block_states, axis=0)
    zero_state = jnp.zeros_like(device_state)
    incoming = entering(device_state, "seq", add_states, zero_state, False)
    state = incoming[None] + jnp.cumsum(block_states, axis=0) - block_states
    state_bf = state.astype(jnp.bfloat16)
    scores = jnp.einsum("nthd,nshd->nhts", queries, key_rows, preferred_element_type=jnp.float32)
    scores = jnp.where(causal[None, None], scores, 0.0).astype(jnp.bfloat16)
    attended = jnp.einsum("nthd,nhde->nthe", queries, state_bf, preferred_element_type=jnp.float32)
    attended = attended + jnp.einsum(
        "nhts,nshe->nthe", scores, values, preferred_element_type=jnp.float32
    )
    attended = attended.reshape(row_count, col_count)
    weighted = gain[None, :] * cotangent.astype(jnp.float32)
    squares = jnp.sum(attended * attended, axis=-1)
    total_sq = lax.psum(squares, "head")
    rms = jnp.sqrt(total_sq / WIDTH + 1e-05)
    output = (gain[None, :] * attended / rms[:, None]).astype(jnp.bfloat16)
    inner = lax.psum(jnp.sum(weighted * attended, axis=-1), "head")
    grad_attended = (
        weighted / rms[:, None] - attended * (inner / (WIDTH * rms * rms * rms))[:, None]
    ).astype(jnp.bfloat16)
    grad_blocks = by_blocks(grad_attended)
    block_grads = jnp.einsum(
        "nthd,nthe->nhde", queries, grad_blocks, preferred_element_type=jnp.float32
    )
    device_grad = jnp.sum(block_grads, axis=0)
    later_grad = entering(device_grad, "seq", add_states, zero_state, True)
    after = later_grad[None] + device_grad[None] - jnp.cumsum(block_grads, axis=0)
    after_bf = after.astype(jnp.bfloat16)
    mixed = jnp.einsum("nthe,nshe->nhts", grad_blocks, values, preferred_element_type=jnp.float32)
    mixed = jnp.where(causal[None, None], mixed, 0.0).astype(jnp.bfloat16)
    grad_q = jnp.einsum(
        "nthe,nhde->nthd", grad_blocks, state_bf, preferred_element_type=jnp.float32
    )
    grad_q = grad_q + jnp.einsum(
        "nhts,nshd->nthd", mixed, key_rows, preferred_element_type=jnp.float32
    )
    grad_k = jnp.einsum("nshe,nhde->nshd", values, after_bf, preferred_element_type=jnp.float32)
    grad_k = grad_k + jnp.einsum(
        "nhts,nthd->nshd", mixed, queries, preferred_element_type=jnp.float32
    )
    grad_v = jnp.einsum("nshd,nhde->nshe", key_rows, after_bf, preferred_element_type=jnp.float32)
    grad_v = grad_v + jnp.einsum(
        "nhts,nthe->nshe", scores, grad_blocks, preferred_element_type=jnp.float32
    )
    grad_u = (
        jnp.stack([grad_q, grad_k, grad_v]).reshape(3, row_count, col_count).astype(jnp.bfloat16)
    )
    right_rim = from_behind(grad_u[:, : tap_count - 1, :], "seq", -1)
    extended_grad = jnp.concatenate([grad_u, right_rim], axis=1).astype(jnp.float32)
    grad_total_in = jnp.zeros((3, row_count, col_count), jnp.float32)
    for offset in range(tap_count):
        grad_total_in = (
            grad_total_in
            + conv_weight[:, offset, None, :] * extended_grad[:, offset : offset + row_count, :]
        )
    return (output, grad_total_in.astype(jnp.bfloat16))


def solution(mesh):
    placed = (P(None, "seq", "head"), P(None, None, "head"), P("head"), P("seq", "head"))
    return jax.shard_map(
        body,
        mesh=mesh,
        in_specs=placed,
        out_specs=(P("seq", "head"), P(None, "seq", "head")),
        check_vma=False,
    )
```

profile of v0, /device:TPU:0, one launch (start us, length us, event | category | flops | bytes accessed | tf_op | source)
XLA Modules:
  0.0 241.4 jit_solution(3161101124645385469)
XLA Ops:
  7.2 0.0 all-gather.5.cloned.1.call-start
  7.2 0.8 slice.46
  8.0 4.9 %collective-permute-start = (bf16[3,2,1024]{2,1,0:T(2,128)(2,1)S(1)}, bf16[3,2,1024]{2,1,0:T(2,128)(2,1)S(1)}, u32[]{:S(2)}, u32[]{:S(2)}) collective-permute-start(bf16[3,2,1024]{2,1,0:T(2,128)(2,1)S(1)} %slice.46), channel_id=1, source_target_pairs={{0,4},{4,8},{8,12},{12,16},{16,20},{20,24},{24,28},{1,5},{5,9},{9,... | collective-permute-start | bytes 36872 | tf_op jit(solution)/shard_map/ppermute | solution.py:14
  12.9 0.9 fusion.11
  13.9 4.6 %copy.44 = bf16[3,512,1024]{1,2,0:T(8,128)(2,1)} copy(bf16[3,512,1024]{2,1,0:T(8,128)(2,1)} %param.8) | data formatting | bytes 6291456 | tf_op args[0]
  18.5 0.0 collective-permute-done
  18.5 0.4 copy.43
  18.9 3.6 %maximum_convert_fusion = f32[3,514,1024]{1,2,0:T(8,128)S(1)} fusion(bf16[3,512,1024]{1,2,0:T(8,128)(2,1)} %copy.44, bf16[3,2,1024]{1,2,0:T(8,128)(2,1)S(1)} %copy.43), kind=kLoop, calls=%fused_computation.16 | loop fusion | flops 6316032 | bytes 9474048 | tf_op jit(solution)/shard_map/convert_element_type | solution.py:42
  22.5 5.7 %fusion.4 = bf16[3,512,1024]{1,2,0:T(8,128)(2,1)S(1)} fusion(f32[3,514,1024]{1,2,0:T(8,128)S(1)} %maximum_convert_fusion, f32[3,1024]{1,0:T(4,128)S(1)} %get-tuple-element.117, f32[3,1024]{1,0:T(4,128)S(1)} %get-tuple-element.118, f32[3,1024]{1,0:T(4,128)S(1)} %bitcast.93), kind=kLoop, calls=%fused_computation.12 | loop fusion | flops 9437184 | bytes 22056960 | tf_op jit(solution)/shard_map/convert_element_type | solution.py:50
  28.3 0.2 fusion.10
  28.5 1.5 fusion.12
  30.0 0.0 all-gather.5.cloned.1.call-update
  30.0 0.0 all-gather.7.cloned.1.call-start
  30.1 0.1 iota_compare_fusion
  30.2 0.7 copy-done.11
  30.8 1.4 select_convert_fusion.1
  32.2 0.0 copy-done.2
  32.2 0.0 copy-start
  32.2 1.9 copy-done
  34.2 2.8 %fusion.13 = f32[8,128,512]{2,1,0:T(8,128)} fusion(bf16[512,8,128]{0,2,1:T(8,128)(2,1)S(1)} %bitcast.73, bf16[8,512,512]{2,1,0:T(8,128)(2,1)S(1)} %select_convert_fusion.1), kind=kOutput, calls=%fused_computation.44 | convolution fusion | flops 536870912 | bytes 7340032 | tf_op jit(solution)/shard_map/nhts,nshe->nthe/dot_general | solution.py:72
  37.0 66.3 %all-gather.5.cloned.1.call-done = f32[64,128,128]{2,1,0:T(8,128)} async-done(((f32[8,128,128]{2,1,0:T(8,128)}), f32[64,128,128]{2,1,0:T(8,128)}) %all-gather.5.cloned.1.call-update) | async-done | bytes 4194320 | tf_op jit(solution)/shard_map/all_gather | solution.py:21
  103.3 1.0 copy-done.10
  104.3 0.1 fusion.7
  104.4 0.0 copy-start.12
  104.4 3.4 %fusion.6 = (f32[512]{0:T(512)S(1)}, f32[8,128,512]{2,1,0:T(8,128)}) fusion(f32[8,128,512]{2,1,0:T(8,128)} %fusion.13, bf16[8,128,128]{2,1,0:T(8,128)(2,1)S(1)} %fusion.7, bf16[512,8,128]{0,2,1:T(8,128)(2,1)S(1)} %bitcast.81), kind=kOutput, calls=%fused_computation.19 | convolution fusion | flops 135790080 | bytes 5507072 | tf_op jit(solution)/shard_map/nthd,nhde->nthe/dot_general | solution.py:71
  107.8 1.9 copy.50
  109.7 0.0 copy-done.12
  109.7 1.6 multiply_reduce_fusion
  111.3 5.8 %all-reduce = (f32[512]{0:T(512)S(1)}, f32[512]{0:T(512)S(1)}) all-reduce(f32[512]{0:T(512)S(1)} %get-tuple-element.115, f32[512]{0:T(512)S(1)} %multiply_reduce_fusion), channel_id=1, replica_groups=mesh['seq'=8,'head'=4] {'head'}, use_global_device_ids=true, to_apply=%region_3.4 | all-reduce | flops 1024 | bytes 8192 | tf_op jit(solution)/shard_map/psum | solution.py:78
  117.2 3.2 %subtract_convert_fusion = (bf16[512,1024]{1,0:T(8,128)(2,1)}, bf16[512,1024]{1,0:T(8,128)(2,1)}) fusion(f32[512,1024]{1,0:T(8,128)S(1)} %copy.50, bf16[512,1024]{1,0:T(8,128)(2,1)} %param.11, f32[512]{0:T(512)S(1)} %get-tuple-element.113, f32[512]{0:T(512)S(1)} %get-tuple-element.114, f32[1024]{0:T(1024)S(1)} %copy-done.12), kind=kLoop, calls=%fused_computation.23 | loop fusion | flops 4718592 | bytes 5251072 | tf_op jit(solution)/shard_map/convert_element_type | solution.py:84
  120.3 1.5 copy.76
  121.8 2.5 %fusion.15 = f32[8,128,128]{2,1,0:T(8,128)} fusion(bf16[512,8,128]{0,2,1:T(8,128)(2,1)} %bitcast.82, bf16[512,8,128]{0,2,1:T(8,128)(2,1)S(1)} %bitcast.68), kind=kOutput, calls=%fused_computation.46 | convolution fusion | flops 134217728 | bytes 2621440 | tf_op jit(solution)/shard_map/nthd,nthe->nhde/dot_general | solution.py:86
  124.3 0.0 all-gather.7.cloned.1.call-update
  124.3 2.4 select_convert_fusion
  126.7 0.0 copy-done.3
  126.7 0.0 copy-start.1
  126.7 1.5 fusion.14
  128.2 1.4 add_convert_fusion.2
  129.6 2.0 fusion.17
  131.7 2.1 fusion.16
  133.8 69.7 %all-gather.7.cloned.1.call-done = f32[64,128,128]{2,1,0:T(8,128)} async-done(((f32[8,128,128]{2,1,0:T(8,128)}), f32[64,128,128]{2,1,0:T(8,128)}) %all-gather.7.cloned.1.call-update) | async-done | bytes 4194320 | tf_op jit(solution)/shard_map/all_gather | solution.py:21
  203.5 8.4 %while.23 = (s32[]{:T(128)}, f32[8,128,128]{2,1,0:T(8,128)S(1)}, s32[]{:T(128)}, f32[8,8,128,128]{3,2,1,0:T(8,128)}, s32[]{:T(128)}, /*index=5*/s32[]{:T(128)}, s32[]{:T(128)}, s32[]{:T(128)}) while((s32[]{:T(128)}, f32[8,128,128]{2,1,0:T(8,128)S(1)}, s32[]{:T(128)}, f32[8,8,128,128]{3,2,1,0:T(8,128)}, s32[]{:T(128)}, /*index=5*/s32[]{:T(128)}, ...), condition=%wide.region_7.8_spmd, body=%wide.region_6.7_spmd.sunk | while | flops 131078 | bytes 1573007 | solution.py:28
  203.5 1.2 bitcast_add_fusion.5
  204.8 1.2 bitcast_add_fusion.5
  206.0 1.2 bitcast_add_fusion.5
  207.1 1.2 bitcast_add_fusion.5
  208.3 1.2 bitcast_add_fusion.5
  209.5 1.2 bitcast_add_fusion.5
  210.7 1.2 bitcast_add_fusion.5
  211.9 0.0 copy-start.8
  211.9 0.0 copy-done.9
  211.9 0.1 fusion.8
  212.0 2.2 add_convert_fusion
  214.2 0.0 copy-start.7
  214.3 0.4 add_convert_fusion.1
  214.7 0.5 copy-done.7
  215.2 0.1 pad_maximum_fusion
  215.4 0.3 copy.61
  215.7 1.3 collective-permute-start.1
  217.0 4.3 %collective-permute-done.1 = bf16[3,2,1024]{2,1,0:T(2,128)(2,1)S(1)} collective-permute-done((bf16[3,2,1024]{2,1,0:T(2,128)(2,1)S(1)}, bf16[3,2,1024]{2,1,0:T(2,128)(2,1)S(1)}, u32[]{:S(2)}, u32[]{:S(2)}) %collective-permute-start.1) | collective-permute-done | bytes 12320 | tf_op jit(solution)/shard_map/ppermute | solution.py:14
  221.2 0.4 copy.62
  221.7 1.6 maximum_convert_fusion.1
  223.3 6.7 %fusion.1 = bf16[3,512,1024]{1,2,0:T(8,128)(2,1)} fusion(f32[3,514,1024]{1,2,0:T(8,128)S(1)} %maximum_convert_fusion.1, f32[3,1024]{1,0:T(4,128)S(1)} %get-tuple-element.117, f32[3,1024]{1,0:T(4,128)S(1)} %get-tuple-element.118, f32[3,1024]{1,0:T(4,128)S(1)} %bitcast.94), kind=kLoop, calls=%fused_computation.6 | loop fusion | flops 9437184 | bytes 22056960 | tf_op jit(solution)/shard_map/convert_element_type | solution.py:120
  229.9 4.6 %copy.63 = bf16[3,512,1024]{2,1,0:T(8,128)(2,1)} copy(bf16[3,512,1024]{1,2,0:T(8,128)(2,1)} %fusion.1) | data formatting | bytes 6291456
  (19 shorter events, 0.1 us)
Async XLA Ops:
  7.2 96.1 %all-gather.5.cloned.1.call-start = ((), (), s32[]{:S(2)}) async-start(), calls=%async_computation | async-start | bytes 4718592 | tf_op jit(solution)/shard_map/all_gather | solution.py:21
  8.0 10.5 %collective-permute-start = (bf16[3,2,1024]{2,1,0:T(2,128)(2,1)S(1)}, bf16[3,2,1024]{2,1,0:T(2,128)(2,1)S(1)}, u32[]{:S(2)}, u32[]{:S(2)}) collective-permute-start(bf16[3,2,1024]{2,1,0:T(2,128)(2,1)S(1)} %slice.46), channel_id=1, source_target_pairs={{0,4},{4,8},{8,12},{12,16},{16,20},{20,24},{24,28},{1,5},{5,9},{9,... | collective-permute-start | bytes 36872 | tf_op jit(solution)/shard_map/ppermute | solution.py:14
  28.5 3.7 %copy-start.2 = (bf16[1,512,1024]{1,2,0:T(8,128)(2,1)}, bf16[1,512,1024]{1,2,0:T(8,128)(2,1)S(1)}, u32[]{:S(2)}) copy-start(bf16[1,512,1024]{1,2,0:T(8,128)(2,1)S(1)} %get-tuple-element.105) | copy-start | bytes 3145732
  28.5 75.9 %copy-start.4 = (bf16[1,512,1024]{1,2,0:T(8,128)(2,1)}, bf16[1,512,1024]{1,2,0:T(8,128)(2,1)S(1)}, u32[]{:S(2)}) copy-start(bf16[1,512,1024]{1,2,0:T(8,128)(2,1)S(1)} %get-tuple-element.106) | copy-start | bytes 3145732
  30.0 173.5 %all-gather.7.cloned.1.call-start = ((), (), s32[]{:S(2)}) async-start(), calls=%async_computation.1 | async-start | bytes 4718592 | tf_op jit(solution)/shard_map/all_gather | solution.py:21
  30.1 0.7 copy-start.11
  32.2 1.9 copy-start
  103.3 1.0 copy-start.10
  104.4 5.3 %copy-start.12 = (f32[1024]{0:T(1024)S(1)}, f32[1024]{0:T(1024)}, u32[]{:S(2)}) copy-start(f32[1024]{0:T(1024)} %param.10) | copy-start | bytes 12292
  124.3 2.4 %copy-start.3 = (bf16[1,512,1024]{1,2,0:T(8,128)(2,1)S(1)}, bf16[1,512,1024]{1,2,0:T(8,128)(2,1)}, u32[]{:S(2)}) copy-start(bf16[1,512,1024]{1,2,0:T(8,128)(2,1)} %copy-done.2) | copy-start | bytes 3145732
  126.7 2.9 %copy-start.1 = (bf16[8,512,512]{2,1,0:T(8,128)(2,1)S(1)}, bf16[8,512,512]{2,1,0:T(8,128)(2,1)}, u32[]{:S(2)}) copy-start(bf16[8,512,512]{2,1,0:T(8,128)(2,1)} %copy-done) | copy-start | bytes 12582916
  129.6 2.1 copy-start.5
  203.5 8.5 %copy-start.9 = (f32[8,128,128]{2,1,0:T(8,128)S(1)}, f32[8,128,128]{2,1,0:T(8,128)}, u32[]{:S(2)}) copy-start(f32[8,128,128]{2,1,0:T(8,128)} %fusion.15) | copy-start | bytes 1572868
  211.9 2.3 copy-start.8
  212.0 3.2 %copy-start.6 = (bf16[8,128,512]{2,1,0:T(8,128)(2,1)S(1)}, bf16[8,128,512]{2,1,0:T(8,128)(2,1)}, u32[]{:S(2)}) copy-start(bf16[8,128,512]{2,1,0:T(8,128)(2,1)} %add_convert_fusion.2) | copy-start | bytes 3145732
  214.2 1.0 copy-start.7
  215.7 5.6 %collective-permute-start.1 = (bf16[3,2,1024]{2,1,0:T(2,128)(2,1)S(1)}, bf16[3,2,1024]{2,1,0:T(2,128)(2,1)S(1)}, u32[]{:S(2)}, u32[]{:S(2)}) collective-permute-start(bf16[3,2,1024]{2,1,0:T(2,128)(2,1)S(1)} %copy.61), channel_id=1, source_target_pairs={{4,0},{8,4},{12,8},{16,12},{20,16},{24,20},{28,24},{5,1},{9,5},{13... | collective-permute-start | bytes 36872 | tf_op jit(solution)/shard_map/ppermute | solution.py:14
Sparse Core Ops, SparseCore 0:
  30.1 73.0 all-gather.4
  124.4 78.9 all-gather.6
where the time goes:
time: 242 us; the launch traced here: 241 us
  waiting for transfers between devices  140 us (58%)
  other arithmetic  30.9 us (13%)
  matrix products  23.6 us (10%)
  local copies, waits for them, and re-layouts  20 us (8%)
  between operations  14.3 us (6%)
  starting transfers between devices  6.24 us (3%)
  blocking collectives  5.85 us (2%)
    all_gather x2, waiting for transfers between devices, entering(): gathered = lax.all_gather(part, axis)  136 us
    unnamed x30, local copies, waits for them, and re-layouts  13.4 us
    add x7, other arithmetic, add_states(): return earlier + later  8.23 us
    convert_element_type x1, other arithmetic, body(): return (output, grad_total_in.astype(jnp.bfloat16))  6.65 us
    ppermute x2, starting transfers between devices, from_behind(): return lax.ppermute(x, axis, pairs)  6.16 us
    psum x1, blocking collectives, body(): total_sq = lax.psum(squares, 'head')  5.85 us
    convert_element_type x1, other arithmetic, body(): convolved = conv_total.astype(jnp.bfloat16)  5.72 us
  transfers between devices with their start and end apart: 4, of which 3 were waited for; matrix products, arithmetic and copies ran while one was open for 8% of the time, Pallas kernels for 0%

commit v1 on v0

v1 whole, which is shorter than its diff:
```python
import jax
import jax.numpy as jnp
from jax import lax
from jax.experimental import pallas as pl
from jax.experimental.pallas import tpu as pltpu
from jax.sharding import PartitionSpec as P

HEAD_DIM = 128
BLOCK = 512
RIM = 8
TAIL = 16
F32 = jnp.float32
BF16 = jnp.bfloat16
MESH = pl.DeviceIdType.MESH


def dot(a, b, ca, cb):
    return lax.dot_general(a, b, (((ca,), (cb,)), ((), ())), preferred_element_type=F32)


def split_of(count):
    inner = 1
    while inner * inner * 4 <= count and count % (inner * 2) == 0:
        inner *= 2
    return count // inner, inner


def lower_mask(rows, cols, shift):
    return lax.broadcasted_iota(jnp.int32, (rows, cols), 0) + shift >= lax.broadcasted_iota(
        jnp.int32, (rows, cols), 1
    )


def upper_mask(rows, cols):
    return lax.broadcasted_iota(jnp.int32, (rows, cols), 0) <= lax.broadcasted_iota(
        jnp.int32, (rows, cols), 1
    )


def make_kernel(n_seq, n_head, rows, cols, taps):
    outer, inner = split_of(n_seq)
    heads = cols // HEAD_DIM
    width = cols * n_head
    half = rows // 2
    groups = rows // HEAD_DIM

    def kernel(
        x_hbm, w_ref, gain_ref, c_hbm, out_hbm, gi_hbm,
        xin, cin, qkv, xs, left, scT, att, stb, s_acc, i_acc,
        stat_s, stat_r, rb, cb, gb, outb, gq, gkv, tail, gib,
        own, xsend, xrecv, zsend, zrecv, hsend, hrecv,
        in_sem, c_sem, out_sem, gi_sem, tail_sem, lsem, xsem_s, xsem_r, zsem_s, zsem_r,
        ssem_s, ssem_r, hsem_s, hsem_r,
    ):
        me = lax.axis_index("seq")
        hd = lax.axis_index("head")
        z = me // inner
        x = lax.rem(me, inner)

        def col(h):
            return pl.ds(pl.multiple_of(h * HEAD_DIM, HEAD_DIM), HEAD_DIM)

        def in_copy(h):
            return pltpu.make_async_copy(
                x_hbm.at[:, :, col(h)], xin.at[:, :, col(h)], in_sem.at[h]
            )

        c_copy = pltpu.make_async_copy(c_hbm, cin, c_sem)

        @pl.loop(0, heads)
        def _(h):
            in_copy(h).start()

        c_copy.start()

        bar = pltpu.get_barrier_semaphore()

        def greet(seq, head):
            pl.semaphore_signal(bar, inc=1, device_id=(seq, head), device_id_type=MESH)

        def peer_x(d):
            return z * inner + lax.rem(x + d, inner)

        def peer_h(d):
            return lax.rem(hd + d, n_head)

        for d in range(1, inner):
            greet(peer_x(d), hd)
        for d in range(1, n_head):
            greet(me, peer_h(d))

        @pl.when(me > 0)
        def _():
            greet(me - 1, hd)

        @pl.when(me < n_seq - 1)
        def _():
            greet(me + 1, hd)

        @pl.when(z > 0)
        def _():
            greet(me - inner, hd)

        @pl.when(z < outer - 1)
        def _():
            greet(me + inner, hd)

        @pl.when(me == 0)
        def _():
            left[...] = jnp.zeros(left.shape, BF16)

        @pl.when(me == n_seq - 1)
        def _():
            hrecv[...] = jnp.zeros(hrecv.shape, BF16)

        @pl.when(z == 0)
        def _():
            zrecv[0] = jnp.zeros(zrecv.shape[1:], BF16)

        @pl.when(z == outer - 1)
        def _():
            zrecv[1] = jnp.zeros(zrecv.shape[1:], BF16)

        xs[:, 0:RIM, :] = jnp.zeros((3, RIM, HEAD_DIM), F32)
        s_acc[...] = jnp.zeros(s_acc.shape, F32)
        i_acc[...] = jnp.zeros(i_acc.shape, F32)

        guests = inner - 1 + n_head - 1
        for there in (me > 0, me < n_seq - 1, z > 0, z < outer - 1):
            guests = guests + there.astype(jnp.int32)
        pl.semaphore_wait(bar, guests)

        left_copy = pltpu.make_async_remote_copy(
            src_ref=x_hbm.at[:, rows - RIM : rows, :],
            dst_ref=left,
            send_sem=lsem.at[0],
            recv_sem=lsem.at[1],
            device_id=(lax.rem(me + 1, n_seq), hd),
            device_id_type=MESH,
        )

        @pl.when(me < n_seq - 1)
        def _():
            left_copy.start()

        def conv_rows(i, h, count):
            total = w_ref[i, 0:1, col(h)] * xs[i, RIM : RIM + count, :]
            for j in range(1, taps):
                total = total + w_ref[i, j : j + 1, col(h)] * xs[i, RIM - j : RIM - j + count, :]
            return total.astype(BF16)

        @pl.loop(0, heads)
        def _(h):
            in_copy(h).wait()
            for i in range(3):
                xs[i, RIM : RIM + rows, :] = xin[i, :, col(h)].astype(F32)
                qkv[i, h] = conv_rows(i, h, rows)

        @pl.when(me > 0)
        def _():
            left_copy.wait_recv()

        def x_copy(way, d, h):
            return pltpu.make_async_remote_copy(
                src_ref=xsend.at[way, h],
                dst_ref=xrecv.at[way, d - 1, h],
                send_sem=xsem_s.at[way, d - 1, h],
                recv_sem=xsem_r.at[way, d - 1, h],
                device_id=(peer_x(d), hd),
                device_id_type=MESH,
            )

        def z_copy(way, h):
            target = jnp.minimum(z + 1, outer - 1) if way == 0 else jnp.maximum(z - 1, 0)
            return pltpu.make_async_remote_copy(
                src_ref=zsend.at[way, h],
                dst_ref=zrecv.at[way, h],
                send_sem=zsem_s.at[way, h],
                recv_sem=zsem_r.at[way, h],
                device_id=(target * inner + x, hd),
                device_id_type=MESH,
            )

        has_prev = (z > 0, z < outer - 1)
        has_next = (z < outer - 1, z > 0)

        def scan_step(way, h):
            part = jnp.zeros((HEAD_DIM, HEAD_DIM), F32)
            total = own[h]
            for d in range(1, inner):
                x_copy(way, d, h).wait_recv()
                got = xrecv[way, d - 1, h].astype(F32)
                total = total + got
                before = (x >= d) if way == 0 else (x < d)
                part = part + got * before.astype(F32)

            @pl.when(has_prev[way])
            def _():
                z_copy(way, h).wait_recv()

            entering = zrecv[way, h].astype(F32)

            @pl.when(has_next[way])
            def _():
                zsend[way, h] = (entering + total).astype(BF16)
                z_copy(way, h).start()

            stb[way, h] = (entering + part).astype(BF16)

        def share(way, h, state):
            own[h] = state
            xsend[way, h] = state.astype(BF16)
            for d in range(1, inner):
                x_copy(way, d, h).start()

        @pl.loop(0, heads)
        def _(h):
            for i in range(3):
                xs[i, 0:RIM, :] = left[i, :, col(h)].astype(F32)
                xs[i, RIM : RIM + TAIL, :] = xin[i, 0:TAIL, col(h)].astype(F32)
                qkv[i, h, 0:TAIL, :] = conv_rows(i, h, TAIL)
            share(0, h, dot(qkv[1, h], qkv[2, h], 0, 0))

        lag = (jnp.minimum(2 + 2 * z, heads), jnp.minimum(2 + 2 * (outer - 1 - z), heads))
        low0 = lower_mask(half, half, 0)
        low1 = lower_mask(half, rows, half)
        up0 = upper_mask(half, rows)
        up1 = upper_mask(half, half)

        @pl.loop(0, heads)
        def _(h):
            q0, q1 = qkv[0, h, 0:half, :], qkv[0, h, half:rows, :]
            k0, k1 = qkv[1, h, 0:half, :], qkv[1, h, half:rows, :]
            k, v, q = qkv[1, h], qkv[2, h], qkv[0, h]
            sc = jnp.where(low0, dot(q0, k0, 1, 1), 0.0).astype(BF16)
            att[h, 0:half, :] = dot(sc, v[0:half], 1, 0)
            sc = jnp.where(low1, dot(q1, k, 1, 1), 0.0).astype(BF16)
            att[h, half:rows, :] = dot(sc, v, 1, 0)
            scT[h, 0:half, :] = jnp.where(up0, dot(k0, q, 1, 1), 0.0).astype(BF16)
            scT[h, half:rows, half:rows] = jnp.where(up1, dot(k1, q1, 1, 1), 0.0).astype(BF16)

            @pl.when(h >= lag[0])
            def _():
                scan_step(0, h - lag[0])

        c_copy.wait()

        @pl.loop(0, heads)
        def _(h):
            @pl.when(h >= heads - lag[0])
            def _():
                scan_step(0, h)

            a = dot(qkv[0, h], stb[0, h], 1, 0) + att[h]
            att[h] = a
            s_acc[...] += a * a
            i_acc[...] += (gain_ref[:, col(h)] * cin[:, col(h)].astype(F32)) * a

        sums = []
        for acc in (s_acc, i_acc):
            for b in range(groups):
                piece = acc[b * HEAD_DIM : (b + 1) * HEAD_DIM, :].T
                sums.append(jnp.sum(piece, axis=0, keepdims=True))
        stat_s[...] = jnp.concatenate(sums, axis=0)

        def s_copy(d):
            return pltpu.make_async_remote_copy(
                src_ref=stat_s,
                dst_ref=stat_r.at[d - 1],
                send_sem=ssem_s.at[d - 1],
                recv_sem=ssem_r.at[d - 1],
                device_id=(me, peer_h(d)),
                device_id_type=MESH,
            )

        for d in range(1, n_head):
            s_copy(d).start()
        stats = stat_s[...]
        for d in range(1, n_head):
            s_copy(d).wait_recv()
            stats = stats + stat_r[d - 1]
        rms = jnp.sqrt(stats[0:groups] / width + 1e-05)
        inv = 1.0 / rms
        coef = stats[groups : 2 * groups] / (width * rms * rms * rms)
        turned = jnp.concatenate([inv, coef], axis=0).T
        for b in range(groups):
            at = slice(b * HEAD_DIM, (b + 1) * HEAD_DIM)
            rb[at, :] = jnp.broadcast_to(turned[:, b : b + 1], (HEAD_DIM, HEAD_DIM))
            cb[at, :] = jnp.broadcast_to(
                turned[:, groups + b : groups + b + 1], (HEAD_DIM, HEAD_DIM)
            )

        @pl.loop(0, heads)
        def _(h):
            weighted = gain_ref[:, col(h)] * cin[:, col(h)].astype(F32)
            g = (weighted * rb[...] - att[h] * cb[...]).astype(BF16)
            gb[h] = g
            share(1, h, dot(qkv[0, h], g, 0, 0))

        def out_copy(h):
            return pltpu.make_async_copy(outb.at[:, col(h)], out_hbm.at[:, col(h)], out_sem.at[h])

        @pl.loop(0, heads)
        def _(h):
            outb[:, col(h)] = (gain_ref[:, col(h)] * att[h] * rb[...]).astype(BF16)
            out_copy(h).start()
            g, q, k, v = gb[h], qkv[0, h], qkv[1, h], qkv[2, h]
            across = dot(g, stb[0, h], 1, 1)
            m = jnp.where(low0, dot(g[0:half], v[0:half], 1, 1), 0.0).astype(BF16)
            gq[h, 0:half, :] = (across[0:half] + dot(m, k[0:half], 1, 0)).astype(BF16)
            m = jnp.where(low1, dot(g[half:rows], v, 1, 1), 0.0).astype(BF16)
            gq[h, half:rows, :] = (across[half:rows] + dot(m, k, 1, 0)).astype(BF16)
            m = jnp.where(up0, dot(v[0:half], g, 1, 1), 0.0).astype(BF16)
            gkv[0, h, 0:half, :] = dot(m, q, 1, 0)
            m = jnp.where(up1, dot(v[half:rows], g[half:rows], 1, 1), 0.0).astype(BF16)
            gkv[0, h, half:rows, :] = dot(m, q[half:rows], 1, 0)
            gkv[1, h, 0:half, :] = dot(scT[h, 0:half, :], g, 1, 0)
            gkv[1, h, half:rows, :] = dot(scT[h, half:rows, half:rows], g[half:rows], 1, 0)

            @pl.when(h >= lag[1])
            def _():
                scan_step(1, h - lag[1])

        def h_copy(h):
            return pltpu.make_async_remote_copy(
                src_ref=hsend.at[h],
                dst_ref=hrecv.at[h],
                send_sem=hsem_s.at[h],
                recv_sem=hsem_r.at[h],
                device_id=(jnp.maximum(me - 1, 0), hd),
                device_id_type=MESH,
            )

        body_rows = rows - TAIL

        def gi_copy(h):
            return pltpu.make_async_copy(
                gib.at[:, 0:body_rows, col(h)], gi_hbm.at[:, 0:body_rows, col(h)], gi_sem.at[h]
            )

        def back_rows(i, h, read, count):
            total = w_ref[i, 0:1, col(h)] * read(0, count)
            for j in range(1, taps):
                total = total + w_ref[i, j : j + 1, col(h)] * read(j, count)
            return total.astype(BF16)

        @pl.loop(0, heads)
        def _(h):
            @pl.when(h >= heads - lag[1])
            def _():
                scan_step(1, h)

            after = stb[1, h]
            gk = (gkv[0, h] + dot(qkv[2, h], after, 1, 1)).astype(BF16)
            gv = (gkv[1, h] + dot(qkv[1, h], after, 1, 0)).astype(BF16)
            for i, grad in enumerate((gq[h], gk, gv)):
                full = grad.astype(F32)
                xs[i, 0:rows, :] = full
                hsend[h, i] = xs[i, 0:RIM, :].astype(BF16)
                tail[h, i, 0:TAIL, :] = xs[i, rows - TAIL : rows, :]

            @pl.when(me > 0)
            def _():
                h_copy(h).start()

            for i in range(3):
                gib[i, 0:body_rows, col(h)] = back_rows(
                    i, h, lambda j, count, i=i: xs[i, j : j + count, :], body_rows
                )
            gi_copy(h).start()

        @pl.loop(0, heads)
        def _(h):
            @pl.when(me < n_seq - 1)
            def _():
                h_copy(h).wait_recv()

            for i in range(3):
                tail[h, i, TAIL : TAIL + RIM, :] = hrecv[h, i].astype(F32)
                gib[i, body_rows:rows, col(h)] = back_rows(
                    i, h, lambda j, count, i=i: tail[h, i, j : j + count, :], TAIL
                )

        tail_copy = pltpu.make_async_copy(
            gib.at[:, body_rows:rows, :], gi_hbm.at[:, body_rows:rows, :], tail_sem
        )
        tail_copy.start()

        @pl.when(me < n_seq - 1)
        def _():
            left_copy.wait_send()

        for d in range(1, n_head):
            s_copy(d).wait_send()

        @pl.loop(0, heads)
        def _(h):
            out_copy(h).wait()
            gi_copy(h).wait()
            for way in range(2):
                for d in range(1, inner):
                    x_copy(way, d, h).wait_send()

                @pl.when(has_next[way])
                def _():
                    z_copy(way, h).wait_send()

            @pl.when(me > 0)
            def _():
                h_copy(h).wait_send()

        tail_copy.wait()

    dma = pltpu.SemaphoreType.DMA
    state = (heads, HEAD_DIM, HEAD_DIM)
    scratch = [
        pltpu.VMEM((3, rows, cols), BF16),
        pltpu.VMEM((rows, cols), BF16),
        pltpu.VMEM((3, heads, rows, HEAD_DIM), BF16),
        pltpu.VMEM((3, rows + RIM, HEAD_DIM), F32),
        pltpu.VMEM((3, RIM, cols), BF16),
        pltpu.VMEM((heads, rows, rows), BF16),
        pltpu.VMEM((heads, rows, HEAD_DIM), F32),
        pltpu.VMEM((2,) + state, BF16),
        pltpu.VMEM((rows, HEAD_DIM), F32),
        pltpu.VMEM((rows, HEAD_DIM), F32),
        pltpu.VMEM((2 * groups, HEAD_DIM), F32),
        pltpu.VMEM((n_head - 1, 2 * groups, HEAD_DIM), F32),
        pltpu.VMEM((rows, HEAD_DIM), F32),
        pltpu.VMEM((rows, HEAD_DIM), F32),
        pltpu.VMEM((heads, rows, HEAD_DIM), BF16),
        pltpu.VMEM((rows, cols), BF16),
        pltpu.VMEM((heads, rows, HEAD_DIM), BF16),
        pltpu.VMEM((2, heads, rows, HEAD_DIM), F32),
        pltpu.VMEM((heads, 3, TAIL + RIM, HEAD_DIM), F32),
        pltpu.VMEM((3, rows, cols), BF16),
        pltpu.VMEM(state, F32),
        pltpu.VMEM((2,) + state, BF16),
        pltpu.VMEM((2, inner - 1) + state, BF16),
        pltpu.VMEM((2,) + state, BF16),
        pltpu.VMEM((2,) + state, BF16),
        pltpu.VMEM((heads, 3, RIM, HEAD_DIM), BF16),
        pltpu.VMEM((heads, 3, RIM, HEAD_DIM), BF16),
        dma((heads,)),
        dma,
        dma((heads,)),
        dma((heads,)),
        dma,
        dma((2,)),
        dma((2, inner - 1, heads)),
        dma((2, inner - 1, heads)),
        dma((2, heads)),
        dma((2, heads)),
        dma((n_head - 1,)),
        dma((n_head - 1,)),
        dma((heads,)),
        dma((heads,)),
    ]
    return kernel, scratch


def solution(mesh):
    n_seq, n_head = mesh.shape["seq"], mesh.shape["head"]

    def body(inputs, conv_weight, gain, cotangent):
        _, rows, cols = inputs.shape
        assert rows == BLOCK and n_seq > 1 and n_head > 1
        kernel, scratch = make_kernel(n_seq, n_head, rows, cols, conv_weight.shape[1])
        hbm = pl.BlockSpec(memory_space=pl.ANY)
        vmem = pl.BlockSpec(memory_space=pltpu.VMEM)
        return pl.pallas_call(
            kernel,
            out_shape=(
                jax.ShapeDtypeStruct((rows, cols), BF16),
                jax.ShapeDtypeStruct((3, rows, cols), BF16),
            ),
            in_specs=[hbm, vmem, vmem, hbm],
            out_specs=(hbm, hbm),
            scratch_shapes=scratch,
            compiler_params=pltpu.CompilerParams(
                collective_id=0, has_side_effects=True, vmem_limit_bytes=56 * 1024 * 1024
            ),
            name="block",
        )(inputs, conv_weight, gain.reshape(1, cols), cotangent)

    placed = (P(None, "seq", "head"), P(None, None, "head"), P("head"), P("seq", "head"))
    return jax.shard_map(
        body,
        mesh=mesh,
        in_specs=placed,
        out_specs=(P("seq", "head"), P(None, "seq", "head")),
        check_vma=False,
    )
```

time: 242 us -> 62.7 us (0.26)
  waiting for transfers between devices: 140 us -> 0 us
  Pallas kernels: 0 us -> 55.7 us
  other arithmetic: 30.9 us -> 0 us
  matrix products: 23.6 us -> 0 us
  local copies, waits for them, and re-layouts: 20 us -> 6.12 us
  between operations: 14.3 us -> 0.64 us
  starting transfers between devices: 6.24 us -> 0 us
  blocking collectives: 5.85 us -> 0 us
    all_gather x2 -> x0, waiting for transfers between devices: 136 us -> none  [entering(): gathered = lax.all_gather(part, axis)]
    pallas_call x0 -> x1, Pallas kernels: none -> 55.7 us  [body(): pl.pallas_call(kernel, out_shape=(jax.ShapeDtypeStruct((rows, cols), BF16...]
    dot_general x12 -> x0, matrix products: 23.6 us -> none  [the longest x1 3.4 us: body(): jnp.einsum('nthd,nhde->nthe', queries, state_bf, preferred_element_type=j...]
    convert_element_type x7 -> x0, other arithmetic: 20.9 us -> none  [the longest x1 6.65 us: body(): return (output, grad_total_in.astype(jnp.bfloat16))]
    add x7 -> x0, other arithmetic: 8.23 us -> none  [add_states(): return earlier + later]
    unnamed x30 -> x2, local copies, waits for them, and re-layouts: 13.4 us -> 6.12 us
    ppermute x2 -> x0, starting transfers between devices: 6.16 us -> none  [from_behind(): return lax.ppermute(x, axis, pairs)]
    psum x1 -> x0, blocking collectives: 5.85 us -> none  [body(): total_sq = lax.psum(squares, 'head')]
  transfers between devices with their start and end apart: 4 -> 0, of which waited for: 3 -> 0; matrix products, arithmetic and copies ran while one was open for 8% -> 0% of each run, Pallas kernels for 0% -> 0%
where the time goes in v1:
time: 62.7 us; the launch traced here: 62.4 us
  Pallas kernels  55.7 us (89%)
  local copies, waits for them, and re-layouts  6.12 us (10%)
  between operations  0.64 us (1%)
    pallas_call x1, Pallas kernels, body(): pl.pallas_call(kernel, out_shape=(jax.ShapeDtypeStruct((rows, cols), BF16...  55.7 us
    unnamed x2, local copies, waits for them, and re-layouts  6.12 us

profile of v1, /device:TPU:0, one launch (start us, length us, event | category | flops | bytes accessed | tf_op | source)
XLA Modules:
  0.0 62.4 jit_solution(5001541946450067803)
XLA Ops:
  0.6 55.7 %block.1 = (bf16[512,1024]{1,0:T(8,128)(2,1)}, bf16[3,512,1024]{2,1,0:T(8,128)(2,1)}) custom-call(bf16[3,512,1024]{2,1,0:T(8,128)(2,1)} %x_hbm.1, f32[3,3,1024]{2,1,0:T(4,128)} %w_ref.1, f32[1,1024]{1,0:T(1,128)} %bitcast.1, bf16[512,1024]{1,0:T(8,128)(2,1)} %c_hbm.1), custom_call_target="tpu_custom_call" | custom-call | tf_op jit(solution)/shard_map/block/pallas_call | solution.py:471
  56.3 2.3 %copy.8 = bf16[512,1024]{1,0:T(8,128)(2,1)} copy(bf16[512,1024]{1,0:T(8,128)(2,1)} %get-tuple-element.4) | data formatting | bytes 2097152
  58.6 3.9 %copy.9 = bf16[3,512,1024]{2,1,0:T(8,128)(2,1)} copy(bf16[3,512,1024]{2,1,0:T(8,128)(2,1)} %get-tuple-element.5) | data formatting | bytes 6291456

commit v2 on v1

--- a/solution.py
+++ b/solution.py
@@ -67,12 +67,6 @@
 
         c_copy = pltpu.make_async_copy(c_hbm, cin, c_sem)
 
-        @pl.loop(0, heads)
-        def _(h):
-            in_copy(h).start()
-
-        c_copy.start()
-
         bar = pltpu.get_barrier_semaphore()
 
         def greet(seq, head):
@@ -104,6 +98,12 @@
         @pl.when(z < outer - 1)
         def _():
             greet(me + inner, hd)
+
+        @pl.loop(0, heads)
+        def _(h):
+            in_copy(h).start()
+
+        c_copy.start()
 
         @pl.when(me == 0)
         def _():
@@ -152,7 +152,7 @@
         @pl.loop(0, heads)
         def _(h):
             in_copy(h).wait()
-            for i in range(3):
+            for i in (1, 2):
                 xs[i, RIM : RIM + rows, :] = xin[i, :, col(h)].astype(F32)
                 qkv[i, h] = conv_rows(i, h, rows)
 
@@ -215,13 +215,13 @@
 
         @pl.loop(0, heads)
         def _(h):
-            for i in range(3):
+            for i in (1, 2):
                 xs[i, 0:RIM, :] = left[i, :, col(h)].astype(F32)
                 xs[i, RIM : RIM + TAIL, :] = xin[i, 0:TAIL, col(h)].astype(F32)
                 qkv[i, h, 0:TAIL, :] = conv_rows(i, h, TAIL)
             share(0, h, dot(qkv[1, h], qkv[2, h], 0, 0))
 
-        lag = (jnp.minimum(2 + 2 * z, heads), jnp.minimum(2 + 2 * (outer - 1 - z), heads))
+        lag = (jnp.minimum(2 + 3 * z, heads), jnp.minimum(1 + 3 * (outer - 1 - z), heads))
         low0 = lower_mask(half, half, 0)
         low1 = lower_mask(half, rows, half)
         up0 = upper_mask(half, rows)
@@ -229,6 +229,9 @@
 
         @pl.loop(0, heads)
         def _(h):
+            xs[0, 0:RIM, :] = left[0, :, col(h)].astype(F32)
+            xs[0, RIM : RIM + rows, :] = xin[0, :, col(h)].astype(F32)
+            qkv[0, h] = conv_rows(0, h, rows)
             q0, q1 = qkv[0, h, 0:half, :], qkv[0, h, half:rows, :]
             k0, k1 = qkv[1, h, 0:half, :], qkv[1, h, half:rows, :]
             k, v, q = qkv[1, h], qkv[2, h], qkv[0, h]
@@ -459,6 +462,16 @@
     return kernel, scratch
 
 
+def place(output, grads, output_hbm, grads_hbm, sem):
+    copies = [pltpu.make_async_copy(output, output_hbm, sem.at[3])]
+    for i in range(3):
+        copies.append(pltpu.make_async_copy(grads.at[i], grads_hbm.at[i], sem.at[i]))
+    for copy in copies:
+        copy.start()
+    for copy in copies:
+        copy.wait()
+
+
 def solution(mesh):
     n_seq, n_head = mesh.shape["seq"], mesh.shape["head"]
 
@@ -466,22 +479,33 @@
         _, rows, cols = inputs.shape
         assert rows == BLOCK and n_seq > 1 and n_head > 1
         kernel, scratch = make_kernel(n_seq, n_head, rows, cols, conv_weight.shape[1])
-        hbm = pl.BlockSpec(memory_space=pl.ANY)
+        anywhere = pl.BlockSpec(memory_space=pl.ANY)
+        hbm = pl.BlockSpec(memory_space=pltpu.HBM)
         vmem = pl.BlockSpec(memory_space=pltpu.VMEM)
-        return pl.pallas_call(
+        shapes = (
+            jax.ShapeDtypeStruct((rows, cols), BF16),
+            jax.ShapeDtypeStruct((3, rows, cols), BF16),
+        )
+        output, grads = pl.pallas_call(
             kernel,
-            out_shape=(
-                jax.ShapeDtypeStruct((rows, cols), BF16),
-                jax.ShapeDtypeStruct((3, rows, cols), BF16),
-            ),
+            out_shape=(pltpu.VMEM((rows, cols), BF16), pltpu.VMEM((3, rows, cols), BF16)),
             in_specs=[hbm, vmem, vmem, hbm],
-            out_specs=(hbm, hbm),
+            out_specs=(anywhere, anywhere),
             scratch_shapes=scratch,
             compiler_params=pltpu.CompilerParams(
-                collective_id=0, has_side_effects=True, vmem_limit_bytes=56 * 1024 * 1024
+                collective_id=0, has_side_effects=True, vmem_limit_bytes=58 * 1024 * 1024
             ),
             name="block",
         )(inputs, conv_weight, gain.reshape(1, cols), cotangent)
+        return pl.pallas_call(
+            place,
+            out_shape=shapes,
+            in_specs=[anywhere, anywhere],
+            out_specs=(hbm, hbm),
+            scratch_shapes=[pltpu.SemaphoreType.DMA((4,))],
+            compiler_params=pltpu.CompilerParams(vmem_limit_bytes=1024 * 1024),
+            name="place",
+        )(output, grads)
 
     placed = (P(None, "seq", "head"), P(None, None, "head"), P("head"), P("seq", "head"))
     return jax.shard_map(

time: 62.7 us -> 59 us (0.941)
  local copies, waits for them, and re-layouts: 6.12 us -> 0 us
  Pallas kernels: 55.7 us -> 58.2 us
    unnamed x2 -> x0, local copies, waits for them, and re-layouts: 6.12 us -> none
    pallas_call x1 -> x2, Pallas kernels: 55.7 us -> 58.2 us  [the longest x1 56.1 us: body(): pl.pallas_call(kernel, out_shape=(pltpu.VMEM((rows, cols), BF16), pltpu.V...]
where the time goes in v2:
time: 59 us; the launch traced here: 58.8 us
  Pallas kernels  58.2 us (99%)
  between operations  0.64 us (1%)
    pallas_call x1, Pallas kernels, body(): pl.pallas_call(kernel, out_shape=(pltpu.VMEM((rows, cols), BF16), pltpu.V...  56.1 us
    pallas_call x1, Pallas kernels, body(): pl.pallas_call(place, out_shape=shapes, in_specs=[anywhere, anywhere], ou...  2.04 us

profile of v2, /device:TPU:0, one launch (start us, length us, event | category | flops | bytes accessed | tf_op | source)
XLA Modules:
  0.0 58.8 jit_solution(503816885611289961)
XLA Ops:
  0.6 56.1 %block.1 = (bf16[512,1024]{1,0:T(8,128)(2,1)S(1)}, bf16[3,512,1024]{2,1,0:T(8,128)(2,1)S(1)}) custom-call(bf16[3,512,1024]{2,1,0:T(8,128)(2,1)} %x_hbm.1, f32[3,3,1024]{2,1,0:T(4,128)} %w_ref.1, f32[1,1024]{1,0:T(1,128)} %bitcast.1, bf16[512,1024]{1,0:T(8,128)(2,1)} %c_hbm.1), custom_call_target="tpu_custom_call" | custom-call | tf_op jit(solution)/shard_map/block/pallas_call | solution.py:489
  56.8 2.0 %place.1 = (bf16[512,1024]{1,0:T(8,128)(2,1)}, bf16[3,512,1024]{2,1,0:T(8,128)(2,1)}) custom-call(bf16[512,1024]{1,0:T(8,128)(2,1)S(1)} %get-tuple-element.4.output, bf16[3,512,1024]{2,1,0:T(8,128)(2,1)S(1)} %get-tuple-element.5.grads), custom_call_target="tpu_custom_call" | custom-call | tf_op jit(solution)/shard_map/place/pallas_call | solution.py:500

commit v3 on v2

--- a/solution.py
+++ b/solution.py
@@ -162,7 +162,7 @@
 
         def x_copy(way, d, h):
             return pltpu.make_async_remote_copy(
-                src_ref=xsend.at[way, h],
+                src_ref=xsend.at[way, d - 1, h],
                 dst_ref=xrecv.at[way, d - 1, h],
                 send_sem=xsem_s.at[way, d - 1, h],
                 recv_sem=xsem_r.at[way, d - 1, h],
@@ -207,11 +207,92 @@
 
             stb[way, h] = (entering + part).astype(BF16)
 
+        def chain_step(way, h):
+            @pl.when(has_prev[way])
+            def _():
+                z_copy(way, h).wait_recv()
+
+            entering = zrecv[way, h].astype(F32)
+            mine = own[h]
+
+            @pl.when(has_next[way])
+            def _():
+                zsend[way, h] = (entering + mine).astype(BF16)
+                z_copy(way, h).start()
+
+            for d in range(1, inner):
+                later = (x + d < inner) if way == 0 else (x + d >= inner)
+                xsend[way, d - 1, h] = (entering + mine * later.astype(F32)).astype(BF16)
+                x_copy(way, d, h).start()
+
+        def join_step(way, h):
+            entering = zrecv[way, h].astype(F32)
+            for d in range(1, inner):
+                x_copy(way, d, h).wait_recv()
+                entering = entering + xrecv[way, d - 1, h].astype(F32)
+            stb[way, h] = entering.astype(BF16)
+
+        def is_odd(h):
+            return lax.rem(h, 2) == 1
+
         def share(way, h, state):
             own[h] = state
-            xsend[way, h] = state.astype(BF16)
-            for d in range(1, inner):
-                x_copy(way, d, h).start()
+
+            @pl.when(jnp.logical_not(is_odd(h)))
+            def _():
+                for d in range(1, inner):
+                    xsend[way, d - 1, h] = state.astype(BF16)
+                    x_copy(way, d, h).start()
+
+            @pl.when(is_odd(h) & jnp.logical_not(has_prev[way]))
+            def _():
+                chain_step(way, h)
+
+        far = (z, outer - 1 - z)
+        lag = (
+            jnp.where(far[0] == 0, 0, jnp.where(far[0] == 1, min(3, heads), heads)),
+            jnp.where(far[1] == 0, 0, jnp.where(far[1] == 1, min(6, heads), heads)),
+        )
+        chain_lag = (
+            jnp.clip(3 * far[0] - 1, 0, heads),
+            jnp.where(far[1] <= 1, min(3, heads), heads),
+        )
+
+        def start_relay(way):
+            @pl.when(jnp.logical_not(has_prev[way]))
+            def _():
+                @pl.loop(0, heads)
+                def _(h):
+                    @pl.when(jnp.logical_not(is_odd(h)))
+                    def _():
+                        scan_step(way, h)
+
+        def relay_some(way, h):
+            ha, hc = h - lag[way], h - chain_lag[way]
+
+            @pl.when((hc >= 0) & is_odd(hc) & has_prev[way])
+            def _():
+                chain_step(way, hc)
+
+            @pl.when((ha >= 0) & (lax.rem(ha, 2) == 0) & has_prev[way])
+            def _():
+                scan_step(way, ha)
+
+        def relay_chains(way):
+            @pl.loop(0, heads)
+            def _(h):
+                @pl.when((h >= heads - chain_lag[way]) & is_odd(h) & has_prev[way])
+                def _():
+                    chain_step(way, h)
+
+        def finish(way, h):
+            @pl.when((h >= heads - lag[way]) & jnp.logical_not(is_odd(h)))
+            def _():
+                scan_step(way, h)
+
+            @pl.when(is_odd(h))
+            def _():
+                join_step(way, h)
 
         @pl.loop(0, heads)
         def _(h):
@@ -221,11 +302,12 @@
                 qkv[i, h, 0:TAIL, :] = conv_rows(i, h, TAIL)
             share(0, h, dot(qkv[1, h], qkv[2, h], 0, 0))
 
-        lag = (jnp.minimum(2 + 3 * z, heads), jnp.minimum(1 + 3 * (outer - 1 - z), heads))
         low0 = lower_mask(half, half, 0)
         low1 = lower_mask(half, rows, half)
         up0 = upper_mask(half, rows)
         up1 = upper_mask(half, half)
+
+        start_relay(0)
 
         @pl.loop(0, heads)
         def _(h):
@@ -242,17 +324,15 @@
             scT[h, 0:half, :] = jnp.where(up0, dot(k0, q, 1, 1), 0.0).astype(BF16)
             scT[h, half:rows, half:rows] = jnp.where(up1, dot(k1, q1, 1, 1), 0.0).astype(BF16)
 
-            @pl.when(h >= lag[0])
-            def _():
-                scan_step(0, h - lag[0])
+            relay_some(0, h)
 
         c_copy.wait()
 
-        @pl.loop(0, heads)
-        def _(h):
-            @pl.when(h >= heads - lag[0])
-            def _():
-                scan_step(0, h)
+        relay_chains(0)
+
+        @pl.loop(0, heads)
+        def _(h):
+            finish(0, h)
 
             a = dot(qkv[0, h], stb[0, h], 1, 0) + att[h]
             att[h] = a
@@ -303,6 +383,8 @@
         def out_copy(h):
             return pltpu.make_async_copy(outb.at[:, col(h)], out_hbm.at[:, col(h)], out_sem.at[h])
 
+        start_relay(1)
+
         @pl.loop(0, heads)
         def _(h):
             outb[:, col(h)] = (gain_ref[:, col(h)] * att[h] * rb[...]).astype(BF16)
@@ -320,9 +402,7 @@
             gkv[1, h, 0:half, :] = dot(scT[h, 0:half, :], g, 1, 0)
             gkv[1, h, half:rows, :] = dot(scT[h, half:rows, half:rows], g[half:rows], 1, 0)
 
-            @pl.when(h >= lag[1])
-            def _():
-                scan_step(1, h - lag[1])
+            relay_some(1, h)
 
         def h_copy(h):
             return pltpu.make_async_remote_copy(
@@ -347,11 +427,11 @@
                 total = total + w_ref[i, j : j + 1, col(h)] * read(j, count)
             return total.astype(BF16)
 
-        @pl.loop(0, heads)
-        def _(h):
-            @pl.when(h >= heads - lag[1])
-            def _():
-                scan_step(1, h)
+        relay_chains(1)
+
+        @pl.loop(0, heads)
+        def _(h):
+            finish(1, h)
 
             after = stb[1, h]
             gk = (gkv[0, h] + dot(qkv[2, h], after, 1, 1)).astype(BF16)
@@ -438,7 +518,7 @@
         pltpu.VMEM((heads, 3, TAIL + RIM, HEAD_DIM), F32),
         pltpu.VMEM((3, rows, cols), BF16),
         pltpu.VMEM(state, F32),
-        pltpu.VMEM((2,) + state, BF16),
+        pltpu.VMEM((2, inner - 1) + state, BF16),
         pltpu.VMEM((2, inner - 1) + state, BF16),
         pltpu.VMEM((2,) + state, BF16),
         pltpu.VMEM((2,) + state, BF16),

time: 59 us -> 55.6 us (0.942)
  Pallas kernels: 58.2 us -> 54.8 us
    pallas_call x1, Pallas kernels: 56.1 us -> 52.8 us  [body(): pl.pallas_call(kernel, out_shape=(pltpu.VMEM((rows, cols), BF16), pltpu.V...]
where the time goes in v3:
time: 55.6 us; the launch traced here: 55.4 us
  Pallas kernels  54.8 us (99%)
  between operations  0.64 us (1%)
    pallas_call x1, Pallas kernels, body(): pl.pallas_call(kernel, out_shape=(pltpu.VMEM((rows, cols), BF16), pltpu.V...  52.8 us
    pallas_call x1, Pallas kernels, body(): pl.pallas_call(place, out_shape=shapes, in_specs=[anywhere, anywhere], ou...  2.04 us

profile of v3, /device:TPU:0, one launch (start us, length us, event | category | flops | bytes accessed | tf_op | source)
XLA Modules:
  0.0 55.4 jit_solution(14935457515227635336)
XLA Ops:
  0.6 52.8 %block.1 = (bf16[512,1024]{1,0:T(8,128)(2,1)S(1)}, bf16[3,512,1024]{2,1,0:T(8,128)(2,1)S(1)}) custom-call(bf16[3,512,1024]{2,1,0:T(8,128)(2,1)} %x_hbm.1, f32[3,3,1024]{2,1,0:T(4,128)} %w_ref.1, f32[1,1024]{1,0:T(1,128)} %bitcast.1, bf16[512,1024]{1,0:T(8,128)(2,1)} %c_hbm.1), custom_call_target="tpu_custom_call" | custom-call | tf_op jit(solution)/shard_map/block/pallas_call | solution.py:569
  53.4 2.0 %place.1 = (bf16[512,1024]{1,0:T(8,128)(2,1)}, bf16[3,512,1024]{2,1,0:T(8,128)(2,1)}) custom-call(bf16[512,1024]{1,0:T(8,128)(2,1)S(1)} %get-tuple-element.4.output, bf16[3,512,1024]{2,1,0:T(8,128)(2,1)S(1)} %get-tuple-element.5.grads), custom_call_target="tpu_custom_call" | custom-call | tf_op jit(solution)/shard_map/place/pallas_call | solution.py:580
